TPU v7x, 256 devices: a whole 4x4x8 slice. The times are simulated.
256 devices in a mesh: cube: 4 (over y), row: 4 (over x), col: 16 (over z, core).
Axes of the slice: x: 4, y: 4, z: 8, core: 2. Of those that a mesh axis runs over, the one named last changes fastest.
Arguments:
- front_entries: float32 [4, 8192, 8192], P('cube', 'row', 'col'), as said below
- child_updates: float32 [4, 2, 4096, 4096], P('cube', None, ('row', 'col')), may hold values from -6 to 6, as said below
- child_index: int32 [4, 2, 64], replicated, may hold values from 0 to 127, as said below
- child_blocks: int32 [4, 2], replicated, may hold values from 32 to 64
Outputs:
- factored: float32 [4, 8192, 8192], P('cube', 'row', 'col')
Inputs may be any that keep to these rules, and one draw needn't show every extreme that they name: `front_entries`: each front is symmetric positive definite in natural numbering. `child_updates`: each contribution block is symmetric. `child_index`: each list names 64 different front blocks; entry t of a list names a front block whose rows lie in a 512-wide block b of front variables with b mod 4 = t div (16).
All inputs are finite; a program needn't handle non-finite values.
Results may differ from a plain program's by a relative error of at most 0.0001.
Values sent between devices are 32-bit elements; how exact they have to be, the bound alone decides.
No kernel may reach another device: no remote copies, remote signals or barrier semaphores. Data moves between devices by JAX's collectives and lax.ppermute only.
A program may use at most 128 MiB of HBM per device.

v0:
```python
import jax
import jax.numpy as jnp
from jax import lax
from jax.sharding import PartitionSpec as P

F = 8192
B = 512
SBLK = 64
CR = 4096
PANELS = 2
HIGHEST_PRECISION = lax.Precision.HIGHEST


def swapped(value, axis, apart):
    mask = 2**apart
    pairs = [(source, source ^ mask) for source in range(lax.axis_size(axis))]
    return lax.ppermute(value, axis, pairs)


def spread_2(block, axis, holder):
    block = jnp.where(lax.axis_index(axis) == holder, block, jnp.zeros_like(block))
    return lax.psum(block, axis)


def storage_position(variable, parts, local_size):
    block = variable // B
    return block % parts * local_size + block // parts * B + variable % B


def natural_variable(local_size, parts, index):
    local = jnp.arange(local_size, dtype=jnp.int32)
    return (local // B * parts + index) * B + local % B


def child_variable(block_lists, offsets):
    return jnp.take(block_lists, offsets // SBLK, axis=1) * SBLK + offsets % SBLK


def solve_panel(rows_in, factor, row_block, panel_step, row_index, root_row, row_slot):
    solved = lax.linalg.triangular_solve(
        factor, rows_in, left_side=False, lower=True, transpose_a=True
    )
    solved = jnp.where((row_block < panel_step)[:, None], 0.0, solved)
    with_pivot = lax.dynamic_update_slice(solved, factor, (row_slot * B, 0))
    return jnp.where(row_index == root_row, with_pivot, solved)


def on_device(front_entries, child_updates, child_index, child_blocks):
    n_row = lax.axis_size("row")
    n_col = lax.axis_size("col")
    row_index = lax.axis_index("row")
    col_index = lax.axis_index("col")
    cube_index = lax.axis_index("cube")
    sibling = jnp.bitwise_xor(cube_index, 1)
    working = front_entries[0]
    rows_here, cols_here = working.shape
    piece_rows = child_updates.shape[2]
    arrived_child = swapped(child_updates[0, 1], "cube", 0)
    pieces = jnp.stack([child_updates[0, 0], arrived_child])
    block_lists = jnp.stack([child_index[cube_index, 0], child_index[sibling, 1]])
    counts = jnp.stack([child_blocks[cube_index, 0], child_blocks[sibling, 1]])
    offsets = jnp.arange(CR, dtype=jnp.int32)
    flat_index = row_index * n_col + col_index
    own_rows = flat_index * piece_rows + jnp.arange(piece_rows, dtype=jnp.int32)
    live_cols = (offsets // SBLK)[None, :] < counts[:, None]
    live_rows = (own_rows // SBLK)[None, :] < counts[:, None]
    values = jnp.where(live_rows[:, :, None] & live_cols[:, None, :], pieces, 0.0)
    col_targets = storage_position(child_variable(block_lists, offsets), n_col, cols_here)

    def widen(child_values, targets):
        return jnp.zeros((piece_rows, F), jnp.float32).at[:, targets].add(child_values)

    spread = jax.vmap(widen)(values, col_targets).reshape(2 * piece_rows, F)
    arrived = lax.all_to_all(spread, "col", split_axis=1, concat_axis=0, tiled=True)
    sources = jnp.arange(n_col, dtype=jnp.int32)
    source_rows = (row_index * n_col + sources)[:, None] * piece_rows + jnp.arange(
        piece_rows, dtype=jnp.int32
    )[None, :]
    natural_rows = child_variable(block_lists, source_rows)
    row_targets = storage_position(jnp.swapaxes(natural_rows, 0, 1), n_row, rows_here).reshape(-1)
    local_rows = row_targets - row_index * rows_here
    working = working.at[local_rows].add(arrived)
    row_block = natural_variable(rows_here, n_row, row_index) // B
    col_block = natural_variable(cols_here, n_col, col_index) // B
    identity = jnp.eye(B, dtype=jnp.float32)
    for panel_step in range(PANELS):
        root_row = panel_step % n_row
        row_slot = panel_step // n_row
        root_col = panel_step % n_col
        col_slot = panel_step // n_col
        diagonal = working[row_slot * B : (row_slot + 1) * B, col_slot * B : (col_slot + 1) * B]
        panel_cols = working
        own_pivot = jnp.where(col_index == root_col, diagonal, identity)
        pivot_block = spread_2(own_pivot, "row", root_row)
        factor = jnp.linalg.cholesky(pivot_block)
        own_lower = solve_panel(
            panel_cols, factor, row_block, panel_step, row_index, root_row, row_slot
        )
        lower_rows = spread_2(own_lower, "col", root_col)
        global_block = 0 + col_index
        block_piece = lax.dynamic_slice_in_dim(lower_rows, global_block // n_row * B, B, 0)
        col_pieces = jnp.where(global_block % n_row == row_index, block_piece, 0.0)
        lower_cols = lax.psum(col_pieces, "row")
        working = working - jnp.dot(
            lower_rows,
            lower_cols.T,
            precision=HIGHEST_PRECISION,
            preferred_element_type=jnp.float32,
        )
        replaced = working.at[:, col_slot * B : (col_slot + 1) * B].set(lower_rows)
        working = jnp.where(col_index == root_col, replaced, working)
    finished = (row_block < PANELS)[:, None] & (col_block >= PANELS)[None, :]
    return jnp.where(finished, 0.0, working)[None]


def solution(mesh):
    in_specs = (P("cube", "row", "col"), P("cube", None, ("row", "col"), None), P(), P())
    out_specs = P("cube", "row", "col")
    return jax.shard_map(
        on_device, mesh=mesh, in_specs=in_specs, out_specs=out_specs, check_vma=False
    )
```

profile of v0, /device:TPU:8, one launch (start us, length us, event | category | flops | bytes accessed | tf_op | source)
XLA Modules:
  0.0 1050.2 jit_solution(9398155492795176346)
XLA Ops:
  16.2 14.1 %gather_fusion.1 = s32[4096,2]{1,0:T(8,128)} fusion(s32[2,64]{0,1:T(8,128)S(1)} %copy.127, s32[4096]{0:T(1024)S(1)} %broadcast_clamp_fusion), kind=kCustom, calls=%fused_computation.1 | custom fusion | bytes 81920 | tf_op jit(solution)/shard_map/jit(_take)/gather | solution.py:36
  30.3 7.2 compare_select_fusion
  51.3 48.2 %scatter_custom_fusion.1 = f32[16384,64]{1,0:T(8,128)} fusion(s32[8192]{0:T(1024)S(1)} %bitcast.172, f32[8192,64]{1,0:T(8,128)} %bitcast.167, f32[]{:T(128)} %constant.447.clone.1), kind=kCustom, calls=%fused_computation.11 | custom fusion | flops 524288 | bytes 4194816
  99.5 8.7 copy.175
  131.0 90.6 %all-to-all-done = f32[128,16,512]{2,0,1:T(8,128)} async-done(((f32[128,16,512]{2,0,1:T(8,128)}), f32[128,16,512]{2,0,1:T(8,128)}, u32[]{:S(2)}, u32[]{:S(2)}) %all-to-all-start) | async-done | bytes 4194336 | tf_op jit(solution)/shard_map/all_to_all | solution.py:74
  221.6 17.4 %scatter_fusion = f32[2048,512]{1,0:T(8,128)} fusion(f32[2048,512]{1,0:T(8,128)} %bitcast.156, s32[2048]{0:T(1024)S(1)} %bitcast.171, f32[2048,512]{1,0:T(8,128)} %bitcast.19), kind=kCustom, calls=%fused_computation.2 | custom fusion | flops 1048576 | bytes 12591104 | tf_op jit(solution)/shard_map/scatter-add | solution.py:82
  247.3 50.5 %all-reduce.8.cloned.1.call-done = f32[512,512]{0,1:T(8,128)} async-done(((f32[512,512]{0,1:T(8,128)}), f32[512,512]{0,1:T(8,128)}) %all-reduce.8.cloned.1.call-update) | async-done | bytes 1048592 | tf_op jit(solution)/shard_map/psum | solution.py:22
  300.8 11.7 %cholesky.286 = f32[128,128]{1,0:T(8,128)S(1)} custom-call(f32[128,128]{1,0:T(8,128)S(1)} %cholesky.426), custom_call_target="Cholesky" | custom-call | tf_op jit(solution)/shard_map/jit(cholesky)/cholesky | solution.py:95
  312.5 9.8 custom-call.27
  323.0 11.7 %cholesky.305 = f32[128,128]{1,0:T(8,128)S(1)} custom-call(f32[128,128]{1,0:T(8,128)S(1)} %cholesky.430), custom_call_target="Cholesky" | custom-call | tf_op jit(solution)/shard_map/jit(cholesky)/cholesky | solution.py:95
  335.1 9.9 custom-call.28
  346.2 11.7 %cholesky.326 = f32[128,128]{1,0:T(8,128)S(1)} custom-call(f32[128,128]{1,0:T(8,128)S(1)} %cholesky.435), custom_call_target="Cholesky" | custom-call | tf_op jit(solution)/shard_map/jit(cholesky)/cholesky | solution.py:95
  358.0 9.8 custom-call.29
  368.6 11.9 %cholesky.343 = f32[128,128]{1,0:T(8,128)S(1)} custom-call(f32[128,128]{1,0:T(8,128)S(1)} %convolution_subtract_fusion.9), custom_call_target="Cholesky" | custom-call | tf_op jit(solution)/shard_map/jit(cholesky)/cholesky | solution.py:95
  385.4 8.3 while.8
  393.6 39.3 %custom-call.30 = f32[4,128,128]{1,2,0:T(8,128)S(1)} custom-call(f32[4,128,128]{2,1,0:T(8,128)S(1)} %get-tuple-element.61), custom_call_target="InvertDiagBlocksLowerTriangular" | custom-call | tf_op jit(solution)/shard_map/triangular_solve/custom-call.3 | solution.py:40
  454.3 122.6 %all-reduce.10.cloned.1.call-done = f32[2048,512]{0,1:T(8,128)} async-done(((f32[2048,512]{0,1:T(8,128)}), f32[2048,512]{0,1:T(8,128)}) %all-reduce.10.cloned.1.call-update) | async-done | bytes 4194320 | tf_op jit(solution)/shard_map/psum | solution.py:22
  579.3 50.9 %all-reduce.12.cloned.1.call-done = f32[512,512]{0,1:T(8,128)} async-done(((f32[512,512]{0,1:T(8,128)}), f32[512,512]{0,1:T(8,128)}) %all-reduce.12.cloned.1.call-update) | async-done | bytes 1048592 | tf_op jit(solution)/shard_map/psum | solution.py:103
  630.2 11.9 %subtract_select_fusion = f32[2048,512]{0,1:T(8,128)S(1)} fusion(f32[2048,512]{0,1:T(8,128)} %all-reduce.10.cloned.1.call-done, f32[2048,512]{0,1:T(8,128)} %copy.139, f32[512,512]{0,1:T(8,128)} %all-reduce.12.cloned.1.call-done, pred[]{:T(512)S(6)} %eq.46), kind=kOutput, calls=%fused_computation.14 | convolution fusion | flops 6444548096 | bytes 13631489 | tf_op jit(solution)/shard_map/dot_general | solution.py:104
  645.6 51.7 %all-reduce.14.cloned.1.call-done = f32[512,512]{0,1:T(8,128)} async-done(((f32[512,512]{0,1:T(8,128)}), f32[512,512]{0,1:T(8,128)}) %all-reduce.14.cloned.1.call-update) | async-done | bytes 1048592 | tf_op jit(solution)/shard_map/psum | solution.py:22
  700.3 11.7 %cholesky.358 = f32[128,128]{1,0:T(8,128)S(1)} custom-call(f32[128,128]{1,0:T(8,128)S(1)} %cholesky.439), custom_call_target="Cholesky" | custom-call | tf_op jit(solution)/shard_map/jit(cholesky)/cholesky | solution.py:95
  712.0 9.8 custom-call.31
  722.5 11.7 %cholesky.377 = f32[128,128]{1,0:T(8,128)S(1)} custom-call(f32[128,128]{1,0:T(8,128)S(1)} %cholesky.443), custom_call_target="Cholesky" | custom-call | tf_op jit(solution)/shard_map/jit(cholesky)/cholesky | solution.py:95
  734.6 10.2 custom-call.32
  745.9 11.7 %cholesky.398 = f32[128,128]{1,0:T(8,128)S(1)} custom-call(f32[128,128]{1,0:T(8,128)S(1)} %cholesky.448), custom_call_target="Cholesky" | custom-call | tf_op jit(solution)/shard_map/jit(cholesky)/cholesky | solution.py:95
  757.8 9.8 custom-call.33
  768.4 11.9 %cholesky.415 = f32[128,128]{1,0:T(8,128)S(1)} custom-call(f32[128,128]{1,0:T(8,128)S(1)} %convolution_subtract_fusion.8), custom_call_target="Cholesky" | custom-call | tf_op jit(solution)/shard_map/jit(cholesky)/cholesky | solution.py:95
  785.8 8.6 while.9
  794.4 39.3 %custom-call.34 = f32[4,128,128]{1,2,0:T(8,128)S(1)} custom-call(f32[4,128,128]{2,1,0:T(8,128)S(1)} %get-tuple-element.62), custom_call_target="InvertDiagBlocksLowerTriangular" | custom-call | tf_op jit(solution)/shard_map/triangular_solve/custom-call.3 | solution.py:40
  848.8 122.5 %all-reduce.16.cloned.1.call-done = f32[2048,512]{0,1:T(8,128)} async-done(((f32[2048,512]{0,1:T(8,128)}), f32[2048,512]{0,1:T(8,128)}) %all-reduce.16.cloned.1.call-update) | async-done | bytes 4194320 | tf_op jit(solution)/shard_map/psum | solution.py:22
  973.6 50.9 %all-reduce.18.cloned.1.call-done = f32[512,512]{0,1:T(8,128)} async-done(((f32[512,512]{0,1:T(8,128)}), f32[512,512]{0,1:T(8,128)}) %all-reduce.18.cloned.1.call-update) | async-done | bytes 1048592 | tf_op jit(solution)/shard_map/psum | solution.py:103
  1024.5 13.3 %select_bitcast_fusion = f32[1,2048,512]{1,2,0:T(8,128)} fusion(f32[2048,512]{0,1:T(8,128)} %all-reduce.16.cloned.1.call-done, f32[2048,512]{0,1:T(8,128)} %copy-done.1, f32[512,512]{0,1:T(8,128)} %all-reduce.18.cloned.1.call-done, pred[]{:T(512)S(6)} %eq.44, pred[2048]{0:T(1024)(128)(4,1)S(1)} %broadcast_compare_fusion.1, pred[512]{0:T(512)(128)(4,1)S(1)} %fusion.135), kind=kOutput, calls=%fused_computation.13 | convolution fusion | flops 6446645248 | bytes 13634049 | tf_op jit(solution)/shard_map/dot_general | solution.py:104
  (202 shorter events, 137.9 us)
Async XLA Ops:
  6.5 4.8 copy-start.3
  11.3 3.4 copy-start.4
  12.5 25.7 %copy-start.6 = (s32[2]{0:T(128)S(1)}, s32[2]{0:T(128)}, u32[]{:S(2)}) copy-start(s32[2]{0:T(128)} %constant.461) | copy-start | bytes 28
  12.5 34.5 %collective-permute-start = (f32[64,4096]{1,0:T(8,128)}, f32[64,4096]{1,0:T(8,128)}, u32[]{:S(2)}, u32[]{:S(2)}) collective-permute-start(f32[64,4096]{1,0:T(8,128)} %get-tuple-element.124), channel_id=1, source_target_pairs={{0,64},{64,0},{128,192},{192,128},{1,65},{65,1},{129,193},{193,129... | collective-permute-start | bytes 3145736 | tf_op jit(solution)/shard_map/ppermute | solution.py:17
  30.3 8.7 copy-start.5
  120.4 101.2 %all-to-all-start = ((f32[128,16,512]{2,0,1:T(8,128)}), f32[128,16,512]{2,0,1:T(8,128)}, u32[]{:S(2)}, u32[]{:S(2)}) async-start(f32[128,16,512]{2,0,1:T(8,128)} %copy.138), calls=%async_computation | async-start | bytes 8388608 | tf_op jit(solution)/shard_map/all_to_all | solution.py:74
  127.3 170.4 %all-reduce.8.cloned.1.call-start = ((), (), s32[]{:S(2)}) async-start(), calls=%async_computation.1 | async-start | bytes 2097152 | tf_op jit(solution)/shard_map/psum | solution.py:22
  246.8 330.1 %all-reduce.10.cloned.1.call-start = ((), (), s32[]{:S(2)}) async-start(), calls=%async_computation.2 | async-start | bytes 8388608 | tf_op jit(solution)/shard_map/psum | solution.py:22
  433.0 6.6 copy-start
  454.3 175.9 %all-reduce.12.cloned.1.call-start = ((), (), s32[]{:S(2)}) async-start(), calls=%async_computation.3 | async-start | bytes 2097152 | tf_op jit(solution)/shard_map/psum | solution.py:103
  579.2 118.0 %all-reduce.14.cloned.1.call-start = ((), (), s32[]{:S(2)}) async-start(), calls=%async_computation.4 | async-start | bytes 2097152 | tf_op jit(solution)/shard_map/psum | solution.py:22
  642.1 2.0 copy-start.1
  645.3 325.9 %all-reduce.16.cloned.1.call-start = ((), (), s32[]{:S(2)}) async-start(), calls=%async_computation.5 | async-start | bytes 8388608 | tf_op jit(solution)/shard_map/psum | solution.py:22
  833.7 5.8 copy-start.2
  848.7 175.8 %all-reduce.18.cloned.1.call-start = ((), (), s32[]{:S(2)}) async-start(), calls=%async_computation.6 | async-start | bytes 2097152 | tf_op jit(solution)/shard_map/psum | solution.py:103
Sparse Core Ops, SparseCore 0:
  246.9 50.8 all-reduce.7
  454.4 122.4 all-reduce.9
  579.4 50.7 all-reduce.11
  645.4 51.7 all-reduce.13
  848.8 122.3 all-reduce.15
  973.7 50.7 all-reduce.17
where the time goes:
time: 1060 us; the launch traced here: 1050 us
  waiting for transfers between devices  540 us (51%)
  other arithmetic  334 us (32%)
  local copies, waits for them, and re-layouts  87.2 us (8%)
  matrix products  59.1 us (6%)
  between operations  19.6 us (2%)
    psum x4, waiting for transfers between devices, spread_2(): return lax.psum(block, axis)  347 us
    another operation x29, other arithmetic, on_device(): factor = jnp.linalg.cholesky(pivot_block)  158 us
    psum x2, waiting for transfers between devices, on_device(): lower_cols = lax.psum(col_pieces, 'row')  102 us
    all_to_all x1, waiting for transfers between devices, on_device(): lax.all_to_all(spread, 'col', split_axis=1, concat_axis=0, tiled=True)  90.6 us
    another operation x5, other arithmetic, solve_panel(): lax.linalg.triangular_solve(factor, rows_in, left_side=False, lower=True,...  78.9 us
    unnamed x4, other arithmetic  51.1 us
    another operation x14, matrix products, solve_panel(): lax.linalg.triangular_solve(factor, rows_in, left_side=False, lower=True,...  29.3 us
    dot_general x2, matrix products, on_device(): jnp.dot(lower_rows, lower_cols.T, precision=HIGHEST_PRECISION, preferred_...  25.2 us
  transfers between devices with their start and end apart: 8, of which 7 were waited for; matrix products, arithmetic and copies ran while one was open for 3% of the time, Pallas kernels for 0%

commit v1 on v0

--- a/solution.py
+++ b/solution.py
@@ -11,6 +11,12 @@
 HIGHEST_PRECISION = lax.Precision.HIGHEST
 
 
+def launch_column(sheet, axis_name):
+    passed = lax.all_gather(sheet, axis_name)
+    arr_out = jnp.sum(passed, axis=0)
+    return arr_out
+
+
 def swapped(value, axis, apart):
     mask = 2**apart
     pairs = [(source, source ^ mask) for source in range(lax.axis_size(axis))]
@@ -19,7 +25,7 @@
 
 def spread_2(block, axis, holder):
     block = jnp.where(lax.axis_index(axis) == holder, block, jnp.zeros_like(block))
-    return lax.psum(block, axis)
+    return launch_column(block, axis)
 
 
 def storage_position(variable, parts, local_size):

time: 1060 us -> 1520 us (1.43)
  waiting for transfers between devices: 540 us -> 957 us
  other arithmetic: 334 us -> 385 us
    all_gather x0 -> x4, waiting for transfers between devices: none -> 768 us  [launch_column(): passed = lax.all_gather(sheet, axis_name)]
    psum x4 -> x0, waiting for transfers between devices: 347 us -> none  [spread_2(): return lax.psum(block, axis)]
    reduce_sum x0 -> x4, other arithmetic: none -> 51.7 us  [launch_column(): arr_out = jnp.sum(passed, axis=0)]
  transfers between devices with their start and end apart: 8 -> 8, of which waited for: 7 -> 7; matrix products, arithmetic and copies ran while one was open for 3% -> 2% of each run, Pallas kernels for 0% -> 0%
where the time goes in v1:
time: 1520 us; the launch traced here: 1510 us
  waiting for transfers between devices  957 us (63%)
  other arithmetic  385 us (25%)
  local copies, waits for them, and re-layouts  73.1 us (5%)
  matrix products  64.4 us (4%)
  between operations  19.5 us (1%)
    all_gather x4, waiting for transfers between devices, launch_column(): passed = lax.all_gather(sheet, axis_name)  768 us
    another operation x29, other arithmetic, on_device(): factor = jnp.linalg.cholesky(pivot_block)  159 us
    psum x2, waiting for transfers between devices, on_device(): lower_cols = lax.psum(col_pieces, 'row')  99.1 us
    all_to_all x1, waiting for transfers between devices, on_device(): lax.all_to_all(spread, 'col', split_axis=1, concat_axis=0, tiled=True)  90.6 us
    another operation x5, other arithmetic, solve_panel(): lax.linalg.triangular_solve(factor, rows_in, left_side=False, lower=True,...  78.9 us
    reduce_sum x4, other arithmetic, launch_column(): arr_out = jnp.sum(passed, axis=0)  51.7 us
    unnamed x4, other arithmetic  51.1 us
    another operation x14, matrix products, solve_panel(): lax.linalg.triangular_solve(factor, rows_in, left_side=False, lower=True,...  36 us
  transfers between devices with their start and end apart: 8, of which 7 were waited for; matrix products, arithmetic and copies ran while one was open for 2% of the time, Pallas kernels for 0%

profile of v1, /device:TPU:8, one launch (start us, length us, event | category | flops | bytes accessed | tf_op | source)
XLA Modules:
  0.0 1510.0 jit_solution(15141569457162950772)
XLA Ops:
  16.2 14.1 gather_fusion.1
  51.3 48.2 %scatter_custom_fusion.1 = f32[16384,64]{1,0:T(8,128)} fusion(s32[8192]{0:T(1024)S(1)} %bitcast.182, f32[8192,64]{1,0:T(8,128)} %bitcast.175, f32[]{:T(128)} %constant.447.clone.1), kind=kCustom, calls=%fused_computation.11 | custom fusion | flops 524288 | bytes 4194816
  99.5 8.7 copy.130
  131.0 90.6 %all-to-all-done = f32[128,16,512]{2,0,1:T(8,128)} async-done(((f32[128,16,512]{2,0,1:T(8,128)}), f32[128,16,512]{2,0,1:T(8,128)}, u32[]{:S(2)}, u32[]{:S(2)}) %all-to-all-start) | async-done | bytes 4194336 | tf_op jit(solution)/shard_map/all_to_all | solution.py:80
  221.6 17.4 %scatter_fusion = f32[2048,512]{1,0:T(8,128)} fusion(f32[2048,512]{1,0:T(8,128)} %bitcast.164, s32[2048]{0:T(1024)S(1)} %bitcast.181, f32[2048,512]{1,0:T(8,128)} %bitcast.19), kind=kCustom, calls=%fused_computation.2 | custom fusion | flops 1048576 | bytes 12591104 | tf_op jit(solution)/shard_map/scatter-add | solution.py:88
  241.9 50.4 %all-gather.9.cloned.1.call-done = f32[2048,512]{1,0:T(8,128)} async-done(((f32[512,512]{1,0:T(8,128)}), f32[2048,512]{1,0:T(8,128)}) %all-gather.9.cloned.1.call-update) | async-done | bytes 4194320 | tf_op jit(solution)/shard_map/all_gather | solution.py:15
  295.6 11.7 cholesky.286
  307.5 9.8 custom-call.27
  318.0 11.7 cholesky.305
  329.7 10.0 custom-call.28
  340.3 11.7 cholesky.326
  352.8 9.8 custom-call.29
  363.2 12.1 cholesky.343
  379.4 8.1 while.8
  387.6 39.3 %custom-call.30 = f32[4,128,128]{1,2,0:T(8,128)S(1)} custom-call(f32[4,128,128]{2,1,0:T(8,128)S(1)} %get-tuple-element.61), custom_call_target="InvertDiagBlocksLowerTriangular" | custom-call | tf_op jit(solution)/shard_map/triangular_solve/custom-call.3 | solution.py:46
  449.7 332.7 %all-gather.11.cloned.1.call-done = f32[32768,512]{1,0:T(8,128)} async-done(((f32[2048,512]{1,0:T(8,128)}), f32[32768,512]{1,0:T(8,128)}) %all-gather.11.cloned.1.call-update) | async-done | bytes 67108880 | tf_op jit(solution)/shard_map/all_gather | solution.py:15
  782.4 23.1 %reduce_sum.37 = f32[2048,512]{1,0:T(8,128)} reduce(f32[16,2048,512]{2,1,0:T(8,128)} %bitcast.33, f32[]{:T(128)} %constant.447.clone.1), dimensions={0}, to_apply=%region_11.14 | reduce | flops 15728640 | bytes 71303168 | tf_op jit(solution)/shard_map/reduce_sum | solution.py:16
  807.9 49.5 %all-reduce.4.cloned.1.call-done = f32[512,512]{1,0:T(8,128)} async-done(((f32[512,512]{1,0:T(8,128)}), f32[512,512]{1,0:T(8,128)}) %all-reduce.4.cloned.1.call-update) | async-done | bytes 1048592 | tf_op jit(solution)/shard_map/psum | solution.py:109
  857.5 11.7 subtract_select_fusion
  872.4 51.8 %all-gather.13.cloned.1.call-done = f32[2048,512]{1,0:T(8,128)} async-done(((f32[512,512]{1,0:T(8,128)}), f32[2048,512]{1,0:T(8,128)}) %all-gather.13.cloned.1.call-update) | async-done | bytes 4194320 | tf_op jit(solution)/shard_map/all_gather | solution.py:15
  927.6 11.7 cholesky.358
  939.5 9.8 custom-call.31
  949.9 11.7 cholesky.377
  963.0 10.2 custom-call.32
  973.9 11.7 cholesky.398
  986.3 9.8 custom-call.33
  996.7 11.8 cholesky.415
  1020.2 39.3 %custom-call.34 = f32[4,128,128]{1,2,0:T(8,128)S(1)} custom-call(f32[4,128,128]{2,1,0:T(8,128)S(1)} %get-tuple-element.62), custom_call_target="InvertDiagBlocksLowerTriangular" | custom-call | tf_op jit(solution)/shard_map/triangular_solve/custom-call.3 | solution.py:46
  1082.3 332.7 %all-gather.15.cloned.1.call-done = f32[32768,512]{1,0:T(8,128)} async-done(((f32[2048,512]{1,0:T(8,128)}), f32[32768,512]{1,0:T(8,128)}) %all-gather.15.cloned.1.call-update) | async-done | bytes 67108880 | tf_op jit(solution)/shard_map/all_gather | solution.py:15
  1415.0 23.1 %reduce_sum.39 = f32[2048,512]{1,0:T(8,128)} reduce(f32[16,2048,512]{2,1,0:T(8,128)} %bitcast.47, f32[]{:T(128)} %constant.447.clone.1), dimensions={0}, to_apply=%region_14.17 | reduce | flops 15728640 | bytes 71303168 | tf_op jit(solution)/shard_map/reduce_sum | solution.py:16
  1440.5 49.5 %all-reduce.6.cloned.1.call-done = f32[512,512]{1,0:T(8,128)} async-done(((f32[512,512]{1,0:T(8,128)}), f32[512,512]{1,0:T(8,128)}) %all-reduce.6.cloned.1.call-update) | async-done | bytes 1048592 | tf_op jit(solution)/shard_map/psum | solution.py:109
  1490.1 12.9 select_bitcast_fusion
  (172 shorter events, 149.9 us)
Async XLA Ops:
  6.5 4.8 copy-start.3
  11.3 3.4 copy-start.4
  12.5 25.7 %copy-start.6 = (s32[2]{0:T(128)S(1)}, s32[2]{0:T(128)}, u32[]{:S(2)}) copy-start(s32[2]{0:T(128)} %constant.461) | copy-start | bytes 28
  12.5 34.5 %collective-permute-start = (f32[64,4096]{1,0:T(8,128)}, f32[64,4096]{1,0:T(8,128)}, u32[]{:S(2)}, u32[]{:S(2)}) collective-permute-start(f32[64,4096]{1,0:T(8,128)} %get-tuple-element.84), channel_id=1, source_target_pairs={{0,64},{64,0},{128,192},{192,128},{1,65},{65,1},{129,193},{193,129... | collective-permute-start | bytes 3145736 | tf_op jit(solution)/shard_map/ppermute | solution.py:23
  30.3 8.7 copy-start.5
  120.4 101.2 %all-to-all-start = ((f32[128,16,512]{2,0,1:T(8,128)}), f32[128,16,512]{2,0,1:T(8,128)}, u32[]{:S(2)}, u32[]{:S(2)}) async-start(f32[128,16,512]{2,0,1:T(8,128)} %copy.106), calls=%async_computation | async-start | bytes 8388608 | tf_op jit(solution)/shard_map/all_to_all | solution.py:80
  127.3 164.9 %all-gather.9.cloned.1.call-start = ((), (), s32[]{:S(2)}) async-start(), calls=%async_computation.3 | async-start | bytes 5242880 | tf_op jit(solution)/shard_map/all_gather | solution.py:15
  241.4 541.0 %all-gather.11.cloned.1.call-start = ((), (), s32[]{:S(2)}) async-start(), calls=%async_computation.4 | async-start | bytes 71303168 | tf_op jit(solution)/shard_map/all_gather | solution.py:15
  387.5 41.6 %copy-start.1 = (f32[512,512]{1,0:T(8,128)}, f32[512,512]{1,0:T(8,128)S(1)}, u32[]{:S(2)}) copy-start(f32[512,512]{1,0:T(8,128)S(1)} %get-tuple-element.225) | copy-start | bytes 3145732
  449.4 408.0 %all-reduce.4.cloned.1.call-start = ((), (), s32[]{:S(2)}) async-start(), calls=%async_computation.1 | async-start | bytes 2097152 | tf_op jit(solution)/shard_map/psum | solution.py:109
  807.9 116.3 %all-gather.13.cloned.1.call-start = ((), (), s32[]{:S(2)}) async-start(), calls=%async_computation.5 | async-start | bytes 5242880 | tf_op jit(solution)/shard_map/all_gather | solution.py:15
  869.2 2.0 copy-start
  872.4 542.7 %all-gather.15.cloned.1.call-start = ((), (), s32[]{:S(2)}) async-start(), calls=%async_computation.6 | async-start | bytes 71303168 | tf_op jit(solution)/shard_map/all_gather | solution.py:15
  1020.2 41.6 %copy-start.2 = (f32[512,512]{1,0:T(8,128)}, f32[512,512]{1,0:T(8,128)S(1)}, u32[]{:S(2)}) copy-start(f32[512,512]{1,0:T(8,128)S(1)} %get-tuple-element.226) | copy-start | bytes 3145732
  1082.1 408.0 %all-reduce.6.cloned.1.call-start = ((), (), s32[]{:S(2)}) async-start(), calls=%async_computation.2 | async-start | bytes 2097152 | tf_op jit(solution)/shard_map/psum | solution.py:109
Sparse Core Ops, SparseCore 0:
  241.5 50.6 all-gather.8
  449.6 332.8 all-gather.10
  808.0 49.4 all-reduce.3
  872.5 51.6 all-gather.12
  1082.2 332.8 all-gather.14
  1440.6 49.4 all-reduce.5
